TPU v7x, 32 devices: a whole 2x2x4 slice. The times are simulated.
32 devices in a mesh: frame: 4 (over y, x), sector: 8 (over z, core).
Axes of the slice: x: 2, y: 2, z: 4, core: 2. Of those that a mesh axis runs over, the one named last changes fastest.
Arguments:
- camera: bfloat16 [4096, 1536], P(('frame', 'sector')), may hold values from -6 to 6
- owners: int32 [256], P(('frame', 'sector')), may hold values from 0 to 7, as said below
- unit_slots: int32 [256, 8], P(('frame', 'sector')), may hold values from 0 to 15, as said below
- pool_weights: bfloat16 [256, 8, 16, 128], P(('frame', 'sector')), may hold values from -0.0234375 to 0.0234375
- student: bfloat16 [32768, 512], P(('frame', 'sector')), may hold values from -0.25 to 0.25
- head_weight: bfloat16 [1536, 512], replicated, may hold values from -0.15625 to 0.15625
Outputs:
- grad_student: bfloat16 [32768, 512], P(('frame', 'sector'))
- grad_head: float32 [1536, 512], P('sector')
Inputs may be any that keep to these rules, and one draw needn't show every extreme that they name: `owners`: in every frame group a device sends at most 2 of its units to any one sector, one sector receives exactly 2 units from every device of the group, and every sector receives at least one unit. `unit_slots`: an entry q of a lidar block held by sector o of frame group f names the unit of rank q % 2 among the units of device q // 2 of group f that are owned by o; that unit exists, and every unit is named by at least one entry of its owner.
All inputs are finite; a program needn't handle non-finite values.
Results may differ from a plain program's by a relative error of at most 0.005.
Values may be sent and summed in bfloat16 or wider, within the bound.
A program may use at most 64 MiB of HBM per device.

v0:
```python
import jax
import jax.numpy as jnp
from jax import lax
from jax.sharding import PartitionSpec as P

CAP = 2


LOSS_WEIGHT = 8.0
EPSILON = 1e-06


def cosine_grads(target, student):
    learner = student.astype(jnp.float32)
    norm_teacher = jnp.sqrt(jnp.sum(target * target, axis=-1, keepdims=True) + EPSILON)
    norm_learner = jnp.sqrt(jnp.sum(learner * learner, axis=-1, keepdims=True) + EPSILON)
    cosine = jnp.sum(target * learner, axis=-1, keepdims=True) / (norm_teacher * norm_learner)
    grad_learner = -LOSS_WEIGHT * (
        target / (norm_teacher * norm_learner) - cosine * learner / (norm_learner * norm_learner)
    )
    grad_teacher = -LOSS_WEIGHT * (
        learner / (norm_teacher * norm_learner) - cosine * target / (norm_teacher * norm_teacher)
    )
    return (grad_teacher.astype(jnp.bfloat16), grad_learner.astype(jnp.bfloat16))


def project_rows(features, head_weight):
    return jnp.dot(features, head_weight, preferred_element_type=jnp.float32).astype(jnp.bfloat16)


def on_device(camera, owners, unit_slots, pool_weights, student, head_weight):
    sectors = lax.axis_size("sector")
    count_units = owners.shape[0]
    unit_rows = camera.shape[0] // count_units
    width = camera.shape[1]
    head_width = head_weight.shape[1]
    blocks, per_block = unit_slots.shape
    block_rows = pool_weights.shape[3]
    earlier = jnp.arange(count_units)[:, None] > jnp.arange(count_units)[None, :]
    matching = owners[:, None] == owners[None, :]
    rank_of = jnp.sum(jnp.where(earlier & matching, 1, 0), axis=1).astype(jnp.int32)
    destination = owners * CAP + rank_of
    placing = (jnp.arange(sectors * CAP)[:, None] == destination[None, :]).astype(jnp.bfloat16)
    flat_slots = unit_slots.reshape(-1)
    packed = jnp.dot(
        placing, camera.reshape(count_units, unit_rows * width), preferred_element_type=jnp.float32
    ).astype(jnp.bfloat16)
    packed = packed.reshape(sectors, CAP, unit_rows, width)
    arrived = lax.all_to_all(packed, "sector", split_axis=0, concat_axis=0, tiled=True).reshape(
        sectors * CAP * unit_rows, width
    )
    slot_proj = project_rows(arrived, head_weight).reshape(sectors * CAP, unit_rows, head_width)
    chosen = jnp.take(slot_proj, flat_slots, axis=0).reshape(
        blocks, per_block, unit_rows, head_width
    )
    target = jnp.einsum(
        "bkjl,bkjh->blh", pool_weights, chosen, preferred_element_type=jnp.float32
    ).reshape(blocks * block_rows, head_width)
    grad_teacher, grad_student = cosine_grads(target, student)
    spread = jnp.einsum(
        "bkjl,blh->bkjh",
        pool_weights,
        grad_teacher.reshape(blocks, block_rows, head_width),
        preferred_element_type=jnp.float32,
    )
    slot_grad = jax.ops.segment_sum(
        spread.reshape(blocks * per_block, unit_rows * head_width),
        flat_slots,
        num_segments=sectors * CAP,
    ).astype(jnp.bfloat16)
    row_grads = slot_grad.reshape(sectors * CAP * unit_rows, head_width)
    sector_sums = lax.psum_scatter(
        lax.dot_general(
            arrived, row_grads, (((0,), (0,)), ((), ())), preferred_element_type=jnp.float32
        ),
        "sector",
        scatter_dimension=0,
        tiled=True,
    )
    grad_head = lax.psum(sector_sums, "frame")
    return (grad_student, grad_head)


def solution(mesh):
    return jax.shard_map(
        on_device,
        mesh=mesh,
        in_specs=(
            P(("frame", "sector"), None),
            P(("frame", "sector")),
            P(("frame", "sector"), None),
            P(("frame", "sector"), None, None, None),
            P(("frame", "sector"), None),
            P(),
        ),
        out_specs=(P(("frame", "sector"), None), P("sector", None)),
        check_vma=False,
    )
```

profile of v0, /device:TPU:0, one launch (start us, length us, event | category | flops | bytes accessed | tf_op | source)
XLA Modules:
  0.0 148.0 jit_solution(6833077229085780709)
XLA Ops:
  7.2 1.3 reshape.112
  8.5 0.9 select_reduce_fusion
  9.4 0.7 multiply_add_fusion
  10.1 0.3 convolution_convert_fusion
  10.4 1.1 copy.10
  11.5 6.3 %all-to-all-start = ((bf16[8,2,16,1536]{3,2,1,0:T(8,128)(2,1)}), bf16[8,2,16,1536]{3,2,1,0:T(8,128)(2,1)S(1)}, u32[]{:S(2)}, u32[]{:S(2)}) async-start(bf16[8,2,16,1536]{3,2,1,0:T(8,128)(2,1)} %bitcast.19), calls=%async_computation | async-start | bytes 1572864 | tf_op jit(solution)/shard_map/all_to_all | solution.py:49
  17.9 0.1 reshape.116
  18.0 0.1 reshape.131
  18.1 20.7 %all-to-all-done = bf16[8,2,16,1536]{3,2,1,0:T(8,128)(2,1)S(1)} async-done(((bf16[8,2,16,1536]{3,2,1,0:T(8,128)(2,1)}), bf16[8,2,16,1536]{3,2,1,0:T(8,128)(2,1)S(1)}, u32[]{:S(2)}, u32[]{:S(2)}) %all-to-all-start) | async-done | bytes 786464 | tf_op jit(solution)/shard_map/all_to_all | solution.py:49
  38.8 0.6 convolution_convert_fusion.1
  39.4 0.3 copy-done.2
  39.7 0.6 gather_fusion
  40.4 0.6 fusion.9
  41.0 0.6 copy-done.1
  41.6 0.4 fusion.1
  42.0 2.2 %fusion.7 = (bf16[1024,512]{1,0:T(8,128)(2,1)S(1)}, bf16[1024,512]{1,0:T(8,128)(2,1)}) fusion(bf16[1024,512]{1,0:T(8,128)(2,1)S(1)} %copy-done.1, f32[8,512,128,1]{1,2,3,0:T(8,128)S(1)} %get-tuple-element.11, f32[1024]{0:T(1024)S(1)} %get-tuple-element.8, f32[1024]{0:T(1024)S(1)} %get-tuple-element.4, f32[1024]{0:T(1024)S(1)} %get-tuple-element.5, ...), kind=kLoop, calls=%fused_computation.14 | loop fusion | flops 6815744 | bytes 5259264 | tf_op jit(solution)/shard_map/convert_element_type | solution.py:24
  44.2 0.4 convolution_bitcast_fusion
  44.6 2.5 %copy.11 = f32[8,8,16,512]{3,1,2,0:T(8,128)} copy(f32[8,8,16,512]{3,2,1,0:T(8,128)S(1)} %convolution_bitcast_fusion) | data formatting | bytes 4194304
  47.2 4.2 %scatter_custom_fusion = f32[16,8192]{1,0:T(8,128)S(1)} fusion(s32[64]{0:T(128)S(1)} %reshape.131, f32[64,8192]{1,0:T(8,128)} %bitcast.55, f32[]{:T(128)} %constant.8.clone.1), kind=kCustom, calls=%fused_computation.27 | custom fusion | flops 524288 | bytes 524800 | tf_op jit(solution)/shard_map/scatter-add | solution.py:66
  51.4 0.1 reshape.120
  51.5 2.3 %fusion.23 = f32[1536,512]{1,0:T(8,128)} fusion(bf16[256,1536]{1,0:T(8,128)(2,1)S(1)} %bitcast.53, bf16[256,512]{1,0:T(8,128)(2,1)S(1)} %reshape.120), kind=kOutput, calls=%fused_computation.47 | convolution fusion | flops 402653184 | bytes 4194304 | tf_op jit(solution)/shard_map/dot_general | solution.py:73
  53.9 39.4 %reduce-scatter.2.cloned.1.call-done = f32[192,512]{1,0:T(8,128)} async-done(((f32[1536,512]{1,0:T(8,128)}), f32[192,512]{1,0:T(8,128)}) %reduce-scatter.2.cloned.1.call-update) | async-done | bytes 393232 | tf_op jit(solution)/shard_map/reduce_scatter | solution.py:72
  93.2 46.1 %all-reduce.2.cloned.1.call-done = f32[192,512]{1,0:T(8,128)} async-done(((f32[192,512]{1,0:T(8,128)}), f32[192,512]{1,0:T(8,128)}) %all-reduce.2.cloned.1.call-update) | async-done | bytes 393232 | tf_op jit(solution)/shard_map/psum | solution.py:80
  139.4 1.8 %copy.13 = f32[192,512]{1,0:T(8,128)} copy(f32[192,512]{1,0:T(8,128)} %all-reduce.2.cloned.1.call-done) | data formatting | bytes 786432
  (19 shorter events, 0.2 us)
Async XLA Ops:
  7.2 31.7 %copy-start = (bf16[1536,512]{1,0:T(8,128)(2,1)S(1)}, bf16[1536,512]{1,0:T(8,128)(2,1)}, u32[]{:S(2)}) copy-start(bf16[1536,512]{1,0:T(8,128)(2,1)} %param.11) | copy-start | bytes 4718596
  10.1 7.8 %copy-start.5 = (s32[8,8]{1,0:T(8,128)S(1)}, s32[8,8]{1,0:T(8,128)}, u32[]{:S(2)}) copy-start(s32[8,8]{1,0:T(8,128)} %param.8) | copy-start | bytes 772
  11.5 27.3 %all-to-all-start = ((bf16[8,2,16,1536]{3,2,1,0:T(8,128)(2,1)}), bf16[8,2,16,1536]{3,2,1,0:T(8,128)(2,1)S(1)}, u32[]{:S(2)}, u32[]{:S(2)}) async-start(bf16[8,2,16,1536]{3,2,1,0:T(8,128)(2,1)} %bitcast.19), calls=%async_computation | async-start | bytes 1572864 | tf_op jit(solution)/shard_map/all_to_all | solution.py:49
  17.9 75.4 %reduce-scatter.2.cloned.1.call-start = ((), (), s32[]{:S(2)}) async-start(), calls=%async_computation.2 | async-start | bytes 3538944 | tf_op jit(solution)/shard_map/reduce_scatter | solution.py:72
  38.8 0.9 copy-start.2
  38.8 1.5 %copy-start.4 = (bf16[8,8,16,128]{3,2,1,0:T(8,128)(2,1)S(1)}, bf16[8,8,16,128]{3,2,1,0:T(8,128)(2,1)}, u32[]{:S(2)}) copy-start(bf16[8,8,16,128]{3,2,1,0:T(8,128)(2,1)} %param.9) | copy-start | bytes 786436
  40.4 1.2 copy-start.1
  44.6 6.9 %copy-start.3 = (bf16[8,2,16,1536]{3,2,1,0:T(8,128)(2,1)S(1)}, bf16[8,2,16,1536]{3,2,1,0:T(8,128)(2,1)}, u32[]{:S(2)}) copy-start(bf16[8,2,16,1536]{3,2,1,0:T(8,128)(2,1)} %copy-done.2) | copy-start | bytes 2359300
  53.8 85.6 %all-reduce.2.cloned.1.call-start = ((), (), s32[]{:S(2)}) async-start(), calls=%async_computation.3 | async-start | bytes 786432 | tf_op jit(solution)/shard_map/psum | solution.py:80
Sparse Core Ops, SparseCore 0:
  53.9 39.2 reduce-scatter.1
  96.2 43.1 all-reduce.1
where the time goes:
time: 148 us
  waiting for transfers between devices  106 us (72%)
  between operations  14.2 us (10%)
  local copies, waits for them, and re-layouts  8.6 us (6%)
  other arithmetic  8.37 us (6%)
  starting transfers between devices  6.41 us (4%)
  matrix products  4.19 us (3%)
    psum x1, waiting for transfers between devices, on_device(): grad_head = lax.psum(sector_sums, 'frame')  46.1 us
    reduce_scatter x1, waiting for transfers between devices, on_device(): lax.psum_scatter(lax.dot_general(arrived, row_grads, (((0,), (0,)), ((),...  39.4 us
    all_to_all x1, waiting for transfers between devices, on_device(): lax.all_to_all(packed, 'sector', split_axis=0, concat_axis=0, tiled=True)  20.7 us
    unnamed x15, local copies, waits for them, and re-layouts  6.41 us
    all_to_all x1, starting transfers between devices, on_device(): lax.all_to_all(packed, 'sector', split_axis=0, concat_axis=0, tiled=True)  6.33 us
    scatter-add x1, other arithmetic, on_device(): jax.ops.segment_sum(spread.reshape(blocks * per_block, unit_rows * head_w...  4.17 us
  transfers between devices with their start and end apart: 3, of which 3 were waited for; matrix products, arithmetic and copies ran while one was open for 0% of the time, Pallas kernels for 0%

commit v1 on v0

v1 whole, which is shorter than its diff:
```python
import functools

import jax
import jax.numpy as jnp
from jax import lax
from jax.experimental import pallas as pl
from jax.experimental.pallas import tpu as pltpu
from jax.sharding import PartitionSpec as P

CAP = 2
LOSS_WEIGHT = 8.0
EPSILON = 1e-06
F32 = jnp.float32
BF16 = jnp.bfloat16


def dot(a, b):
    return jnp.dot(a, b, preferred_element_type=F32)


def kernel_body(
    sizes,
    owners,
    slots,
    cam_h,
    pool_h,
    stu_h,
    w_h,
    gs_h,
    gh,
    cam,
    pool,
    stu,
    w,
    send,
    recv,
    camt,
    camg,
    bmat,
    bt,
    gt,
    gsv,
    sg,
    back,
    gall,
    acc,
    rsend,
    rrecv,
    fgat,
    load_sem,
    store_sem,
    fs,
    fr,
    cs,
    cr,
    bs,
    br,
    gs_sem,
    gr_sem,
    ps,
    pr,
    xs,
    xr,
    ys,
    yr,
):
    n, nf, units, unit, blocks, refs, lbr, fused = sizes
    rows, width = cam.shape
    head = w.shape[1]
    slot_rows = n * CAP * unit
    part = width // n
    me = lax.axis_index("sector")
    mf = lax.axis_index("frame")

    loads = [
        pltpu.make_async_copy(src, dst, load_sem.at[i])
        for i, (src, dst) in enumerate(((cam_h, cam), (w_h, w), (pool_h, pool), (stu_h, stu)))
    ]
    for copy in loads:
        copy.start()

    def remote(src, dst, ssem, rsem, frame, sector):
        return pltpu.make_async_remote_copy(
            src_ref=src,
            dst_ref=dst,
            send_sem=ssem,
            recv_sem=rsem,
            device_id=(frame, sector),
            device_id_type=pl.DeviceIdType.MESH,
        )

    barrier = pltpu.get_barrier_semaphore()
    for i in range(1, n):
        pl.semaphore_signal(
            barrier, inc=1, device_id=(mf, lax.rem(me + i, n)), device_id_type=pl.DeviceIdType.MESH
        )
    greeted = n - 1
    if fused:
        for i in range(1, nf):
            pl.semaphore_signal(
                barrier,
                inc=1,
                device_id=(lax.rem(mf + i, nf), me),
                device_id_type=pl.DeviceIdType.MESH,
            )
        greeted += nf - 1

    dest = []
    for u in range(units):
        rank = jnp.int32(0)
        for v in range(u):
            rank = rank + jnp.where(owners[v] == owners[u], 1, 0).astype(jnp.int32)
        dest.append(owners[u] * CAP + rank)

    column = lax.broadcasted_iota(jnp.int32, (1, rows), 1)
    place_row = lax.rem(column, unit)
    for u in range(units):
        place_row = place_row + jnp.where(column // unit == u, dest[u] * unit, 0)
    place = (
        lax.broadcasted_iota(jnp.int32, (slot_rows, rows), 0) == place_row
    ).astype(F32).astype(BF16)

    loads[0].wait()
    loads[1].wait()
    projected = dot(cam[...], w[...]).astype(BF16)
    placed = dot(place, projected).astype(BF16).reshape(n, CAP * unit, head)
    send[...] = placed
    pl.semaphore_wait(barrier, greeted)
    forward = []
    for i in range(1, n):
        peer = lax.rem(me + i, n)
        copy = remote(send.at[peer], recv.at[me], fs.at[i], fr.at[i], mf, peer)
        copy.start()
        forward.append(copy)
    recv[me] = send[me]

    for i in range(0, width, 128):
        camt[i : i + 128, :] = cam[:, i : i + 128].T
    columns = []
    for i in range(1, n):
        peer = lax.rem(me + i, n)
        start = pl.multiple_of(peer * part, 16)
        copy = remote(camt.at[pl.ds(start, part)], camg.at[me], cs.at[i], cr.at[i], mf, peer)
        copy.start()
        columns.append(copy)
    camg[me] = camt[pl.ds(pl.multiple_of(me * part, 16), part), :]

    loads[2].wait()
    depth = refs * unit
    ref_column = lax.broadcasted_iota(jnp.int32, (1, depth), 1)
    slot_row = lax.broadcasted_iota(jnp.int32, (slot_rows, depth), 0)
    for b in range(blocks):
        wanted = lax.rem(ref_column, unit)
        for k in range(refs):
            wanted = wanted + jnp.where(ref_column // unit == k, slots[b, k] * unit, 0)
        pick = (slot_row == wanted).astype(F32).astype(BF16)
        combined = dot(pick, pool[b * depth : (b + 1) * depth, :])
        bmat[:, b * lbr : (b + 1) * lbr] = combined.astype(BF16)
        bt[b * lbr : (b + 1) * lbr, :] = combined.T.astype(BF16)

    loads[3].wait()
    for copy in forward:
        copy.wait_recv()
    arrived = recv[...].reshape(slot_rows, head)
    stores = []
    for b in range(blocks):
        span = slice(b * lbr, (b + 1) * lbr)
        target = dot(bt[span, :], arrived)
        learner = stu[span, :].astype(F32)
        inv_t = lax.rsqrt(jnp.sum(target * target, axis=1, keepdims=True) + EPSILON)
        inv_l = lax.rsqrt(jnp.sum(learner * learner, axis=1, keepdims=True) + EPSILON)
        both = inv_t * inv_l
        cosine = jnp.sum(target * learner, axis=1, keepdims=True) * both
        scale = -LOSS_WEIGHT * both
        back_l = LOSS_WEIGHT * cosine * (inv_l * inv_l)
        back_t = LOSS_WEIGHT * cosine * (inv_t * inv_t)
        gsv[span, :] = (target * scale + learner * back_l).astype(BF16)
        gt[span, :] = (learner * scale + target * back_t).astype(BF16)
        store = pltpu.make_async_copy(gsv.at[span], gs_h.at[span], store_sem.at[b])
        store.start()
        stores.append(store)

    sg[...] = dot(bmat[...], gt[...]).astype(BF16).reshape(n, CAP * unit, head)
    returns = []
    for i in range(1, n):
        peer = lax.rem(me + i, n)
        copy = remote(sg.at[peer], back.at[me], bs.at[i], br.at[i], mf, peer)
        copy.start()
        returns.append(copy)
    back[me] = sg[me]

    place_column = lax.broadcasted_iota(jnp.int32, (rows, 1), 0)
    home_row = lax.rem(place_column, unit)
    for u in range(units):
        home_row = home_row + jnp.where(place_column // unit == u, dest[u] * unit, 0)
    home = (
        lax.broadcasted_iota(jnp.int32, (rows, slot_rows), 1) == home_row
    ).astype(F32).astype(BF16)
    for copy in returns:
        copy.wait_recv()
    gall[me] = dot(home, back[...].reshape(slot_rows, head)).astype(BF16)

    nz = n // 2
    z = me // 2
    core = lax.rem(me, 2)
    twin = z * 2 + (1 - core)
    gathers = [None]
    for i in range(1, nz):
        peer = lax.rem(z + i, nz) * 2 + core
        copy = remote(gall.at[me], gall.at[me], gs_sem.at[i], gr_sem.at[i], mf, peer)
        copy.start()
        gathers.append(copy)
    passed = [remote(gall.at[me], gall.at[me], ps.at[0], pr.at[0], mf, twin)]
    passed[0].start()
    for copy in columns:
        copy.wait_recv()
    acc[...] = dot(camg[me], gall[me])
    for i in range(1, nz):
        source = lax.rem(z + nz - i, nz) * 2 + core
        gathers[i].wait_recv()
        copy = remote(gall.at[source], gall.at[source], ps.at[i], pr.at[i], mf, twin)
        copy.start()
        passed.append(copy)
        acc[...] += dot(camg[source], gall[source])
    for i in range(nz):
        source = lax.rem(z + nz - i, nz) * 2 + (1 - core)
        passed[i].wait_recv()
        acc[...] += dot(camg[source], gall[source])

    pending = forward + columns + returns + gathers[1:] + passed
    if fused:
        quarter = part // nf
        rsend[...] = acc[...].astype(BF16)
        sums = []
        for i in range(1, nf):
            peer = lax.rem(mf + i, nf)
            start = pl.multiple_of(peer * quarter, 16)
            copy = remote(
                rsend.at[pl.ds(start, quarter)], rrecv.at[i], xs.at[i], xr.at[i], peer, me
            )
            copy.start()
            sums.append(copy)
        total = acc[pl.ds(pl.multiple_of(mf * quarter, 16), quarter), :]
        for i in range(1, nf):
            sums[i - 1].wait_recv()
            total = total + rrecv[i].astype(F32)
        fgat[mf] = total.astype(BF16)
        spreads = []
        for i in range(1, nf):
            peer = lax.rem(mf + i, nf)
            copy = remote(fgat.at[mf], fgat.at[mf], ys.at[i], yr.at[i], peer, me)
            copy.start()
            spreads.append(copy)
        for copy in spreads:
            copy.wait_recv()
        for f in range(nf):
            gh[f * quarter : (f + 1) * quarter, :] = fgat[f].astype(F32)
        pending = pending + sums + spreads
    else:
        gh[...] = acc[...]
    for copy in pending:
        copy.wait_send()
    for store in stores:
        store.wait()


def on_device(camera, owners, unit_slots, pool_weights, student, head_weight):
    n = lax.axis_size("sector")
    nf = lax.axis_size("frame")
    units = owners.shape[0]
    rows, width = camera.shape
    unit = rows // units
    head = head_weight.shape[1]
    blocks, refs = unit_slots.shape
    lbr = pool_weights.shape[3]
    tokens = blocks * lbr
    slot_rows = n * CAP * unit
    part = width // n
    fused = part % (nf * 16) == 0
    quarter = part // nf if fused else 16
    sizes = (n, nf, units, unit, blocks, refs, lbr, fused)
    any_space = pl.BlockSpec(memory_space=pl.ANY)
    smem = pl.BlockSpec(memory_space=pltpu.SMEM)
    dma = pltpu.SemaphoreType.DMA
    grad_student, grad_head = pl.pallas_call(
        functools.partial(kernel_body, sizes),
        out_shape=(
            jax.ShapeDtypeStruct((tokens, head), BF16),
            jax.ShapeDtypeStruct((part, head), F32),
        ),
        in_specs=[smem, smem, any_space, any_space, any_space, any_space],
        out_specs=(any_space, pl.BlockSpec(memory_space=pltpu.VMEM)),
        scratch_shapes=[
            pltpu.VMEM((rows, width), BF16),
            pltpu.VMEM((blocks * refs * unit, lbr), BF16),
            pltpu.VMEM((tokens, head), BF16),
            pltpu.VMEM((width, head), BF16),
            pltpu.VMEM((n, CAP * unit, head), BF16),
            pltpu.VMEM((n, CAP * unit, head), BF16),
            pltpu.VMEM((width, rows), BF16),
            pltpu.VMEM((n, part, rows), BF16),
            pltpu.VMEM((slot_rows, tokens), BF16),
            pltpu.VMEM((tokens, slot_rows), BF16),
            pltpu.VMEM((tokens, head), BF16),
            pltpu.VMEM((tokens, head), BF16),
            pltpu.VMEM((n, CAP * unit, head), BF16),
            pltpu.VMEM((n, CAP * unit, head), BF16),
            pltpu.VMEM((n, rows, head), BF16),
            pltpu.VMEM((part, head), F32),
            pltpu.VMEM((part, head), BF16),
            pltpu.VMEM((nf, quarter, head), BF16),
            pltpu.VMEM((nf, quarter, head), BF16),
            dma((4,)),
            dma((blocks,)),
            dma((n,)),
            dma((n,)),
            dma((n,)),
            dma((n,)),
            dma((n,)),
            dma((n,)),
            dma((n,)),
            dma((n,)),
            dma((n,)),
            dma((n,)),
            dma((nf,)),
            dma((nf,)),
            dma((nf,)),
            dma((nf,)),
        ],
        compiler_params=pltpu.CompilerParams(
            collective_id=0, has_side_effects=True, vmem_limit_bytes=48 * 1024 * 1024
        ),
    )(
        owners,
        unit_slots,
        camera,
        pool_weights.reshape(blocks * refs * unit, lbr),
        student,
        head_weight,
    )
    if not fused:
        grad_head = lax.psum(grad_head, "frame")
    return (grad_student, grad_head)


def solution(mesh):
    return jax.shard_map(
        on_device,
        mesh=mesh,
        in_specs=(
            P(("frame", "sector"), None),
            P(("frame", "sector")),
            P(("frame", "sector"), None),
            P(("frame", "sector"), None, None, None),
            P(("frame", "sector"), None),
            P(),
        ),
        out_specs=(P(("frame", "sector"), None), P("sector", None)),
        check_vma=False,
    )
```

time: 148 us -> 57.7 us (0.39)
  waiting for transfers between devices: 106 us -> 0 us
  Pallas kernels: 0 us -> 49.2 us
  between operations: 14.2 us -> 0.65 us
  other arithmetic: 8.37 us -> 0 us
  starting transfers between devices: 6.41 us -> 0 us
  matrix products: 4.19 us -> 0 us
    pallas_call x0 -> x1, Pallas kernels: none -> 49.2 us  [on_device(): pl.pallas_call(functools.partial(kernel_body, sizes), out_shape=(jax.Shap...]
    psum x1 -> x0, waiting for transfers between devices: 46.1 us -> none  [on_device(): grad_head = lax.psum(sector_sums, 'frame')]
    reduce_scatter x1 -> x0, waiting for transfers between devices: 39.4 us -> none  [on_device(): lax.psum_scatter(lax.dot_general(arrived, row_grads, (((0,), (0,)), ((),...]
    all_to_all x1 -> x0, waiting for transfers between devices: 20.7 us -> none  [on_device(): lax.all_to_all(packed, 'sector', split_axis=0, concat_axis=0, tiled=True)]
    all_to_all x1 -> x0, starting transfers between devices: 6.33 us -> none  [on_device(): lax.all_to_all(packed, 'sector', split_axis=0, concat_axis=0, tiled=True)]
    dot_general x5 -> x0, matrix products: 4.19 us -> none  [the longest x1 2.26 us: on_device(): lax.dot_general(arrived, row_grads, (((0,), (0,)), ((), ())), preferred_e...]
    scatter-add x1 -> x0, other arithmetic: 4.17 us -> none  [on_device(): jax.ops.segment_sum(spread.reshape(blocks * per_block, unit_rows * head_w...]
    convert_element_type x2 -> x0, other arithmetic: 2.18 us -> none  [the longest x1 2.15 us: cosine_grads(): grad_teacher.astype(jnp.bfloat16)]
  transfers between devices with their start and end apart: 3 -> 0, of which waited for: 3 -> 0; matrix products, arithmetic and copies ran while one was open for 0% -> 0% of each run, Pallas kernels for 0% -> 0%
where the time goes in v1:
time: 57.7 us; the launch traced here: 57.5 us
  Pallas kernels  49.2 us (85%)
  local copies, waits for them, and re-layouts  7.63 us (13%)
  between operations  0.65 us (1%)
    pallas_call x1, Pallas kernels, on_device(): pl.pallas_call(functools.partial(kernel_body, sizes), out_shape=(jax.Shap...  49.2 us
    unnamed x14, local copies, waits for them, and re-layouts  7.63 us

profile of v1, /device:TPU:0, one launch (start us, length us, event | category | flops | bytes accessed | tf_op | source)
XLA Modules:
  0.0 57.5 jit_solution(11592730388521511958)
XLA Ops:
  0.6 0.0 copy-start
  0.6 1.4 %copy-done = bf16[1536,512]{1,0:T(8,128)(2,1)S(1)} copy-done((bf16[1536,512]{1,0:T(8,128)(2,1)S(1)}, bf16[1536,512]{1,0:T(8,128)(2,1)}, u32[]{:S(2)}) %copy-start) | copy-done | bytes 1572888
  2.0 0.0 copy-start.1
  2.0 1.2 %copy-done.1 = bf16[1024,512]{1,0:T(8,128)(2,1)S(1)} copy-done((bf16[1024,512]{1,0:T(8,128)(2,1)S(1)}, bf16[1024,512]{1,0:T(8,128)(2,1)}, u32[]{:S(2)}) %copy-start.1) | copy-done | bytes 1048600
  3.3 0.0 copy-start.2
  3.3 1.0 %copy-done.2 = bf16[128,1536]{1,0:T(8,128)(2,1)S(1)} copy-done((bf16[128,1536]{1,0:T(8,128)(2,1)S(1)}, bf16[128,1536]{1,0:T(8,128)(2,1)}, u32[]{:S(2)}) %copy-start.2) | copy-done | bytes 393240
  4.3 0.0 copy-start.3
  4.3 0.9 %copy-done.3 = bf16[8,8,16,128]{3,2,1,0:T(8,128)(2,1)S(1)} copy-done((bf16[8,8,16,128]{3,2,1,0:T(8,128)(2,1)S(1)}, bf16[8,8,16,128]{3,2,1,0:T(8,128)(2,1)}, u32[]{:S(2)}) %copy-start.3) | copy-done | bytes 262168
  5.2 0.0 copy-start.4
  5.2 0.7 %copy-done.4 = s32[8,8]{1,0:T(8,128)S(1)} copy-done((s32[8,8]{1,0:T(8,128)S(1)}, s32[8,8]{1,0:T(8,128)}, u32[]{:S(2)}) %copy-start.4) | copy-done | bytes 280
  5.9 0.0 copy-start.5
  5.9 0.7 %copy-done.5 = s32[8]{0:T(128)S(1)} copy-done((s32[8]{0:T(128)S(1)}, s32[8]{0:T(128)}, u32[]{:S(2)}) %copy-start.5) | copy-done | bytes 56
  6.6 49.2 %shard_map.77 = (bf16[1024,512]{1,0:T(8,128)(2,1)S(1)}, f32[192,512]{1,0:T(8,128)S(1)}) custom-call(s32[8]{0:T(128)S(1)} %copy-done.5, s32[8,8]{1,0:T(8,128)S(1)} %copy-done.4, bf16[128,1536]{1,0:T(8,128)(2,1)S(1)} %copy-done.2, bf16[1024,128]{1,0:T(8,128)(2,1)S(1)} %bitcast.1, bf16[1024,512]{1,0:T(8,128)(2,1)S(1)} %copy-done.1, bf16[1536,512]{1,0:T(8,128)(2,1)S(1)} %copy-done), custom_call_target="tpu_custom_call" | custom-call | tf_op jit(solution)/shard_map/pallas_call | solution.py:285
  55.7 1.0 %copy.10 = bf16[1024,512]{1,0:T(8,128)(2,1)} copy(bf16[1024,512]{1,0:T(8,128)(2,1)S(1)} %get-tuple-element.4) | data formatting | bytes 2097152
  56.7 0.7 %copy.11 = f32[192,512]{1,0:T(8,128)} copy(f32[192,512]{1,0:T(8,128)S(1)} %get-tuple-element.5) | data formatting | bytes 786432
Async XLA Ops:
  0.6 1.4 %copy-start = (bf16[1536,512]{1,0:T(8,128)(2,1)S(1)}, bf16[1536,512]{1,0:T(8,128)(2,1)}, u32[]{:S(2)}) copy-start(bf16[1536,512]{1,0:T(8,128)(2,1)} %w_h.1) | copy-start | bytes 4718596
  2.0 1.2 %copy-start.1 = (bf16[1024,512]{1,0:T(8,128)(2,1)S(1)}, bf16[1024,512]{1,0:T(8,128)(2,1)}, u32[]{:S(2)}) copy-start(bf16[1024,512]{1,0:T(8,128)(2,1)} %stu_h.1) | copy-start | bytes 3145732
  3.3 1.0 %copy-start.2 = (bf16[128,1536]{1,0:T(8,128)(2,1)S(1)}, bf16[128,1536]{1,0:T(8,128)(2,1)}, u32[]{:S(2)}) copy-start(bf16[128,1536]{1,0:T(8,128)(2,1)} %cam_h.1) | copy-start | bytes 1179652
  4.3 0.9 %copy-start.3 = (bf16[8,8,16,128]{3,2,1,0:T(8,128)(2,1)S(1)}, bf16[8,8,16,128]{3,2,1,0:T(8,128)(2,1)}, u32[]{:S(2)}) copy-start(bf16[8,8,16,128]{3,2,1,0:T(8,128)(2,1)} %param.9) | copy-start | bytes 786436
  5.2 0.7 %copy-start.4 = (s32[8,8]{1,0:T(8,128)S(1)}, s32[8,8]{1,0:T(8,128)}, u32[]{:S(2)}) copy-start(s32[8,8]{1,0:T(8,128)} %slots.1) | copy-start | bytes 772
  5.9 0.7 %copy-start.5 = (s32[8]{0:T(128)S(1)}, s32[8]{0:T(128)}, u32[]{:S(2)}) copy-start(s32[8]{0:T(128)} %owners.1) | copy-start | bytes 100

commit v2 on v1

--- a/solution.py
+++ b/solution.py
@@ -44,8 +44,13 @@
     back,
     gall,
     acc,
-    rsend,
-    rrecv,
+    give,
+    got,
+    keep,
+    fsend,
+    frecv,
+    zsend,
+    zrecv,
     fgat,
     load_sem,
     store_sem,
@@ -59,8 +64,12 @@
     gr_sem,
     ps,
     pr,
+    es,
+    er,
     xs,
     xr,
+    zs,
+    zr,
     ys,
     yr,
 ):
@@ -137,13 +146,14 @@
     for i in range(0, width, 128):
         camt[i : i + 128, :] = cam[:, i : i + 128].T
     columns = []
-    for i in range(1, n):
-        peer = lax.rem(me + i, n)
-        start = pl.multiple_of(peer * part, 16)
-        copy = remote(camt.at[pl.ds(start, part)], camg.at[me], cs.at[i], cr.at[i], mf, peer)
-        copy.start()
-        columns.append(copy)
-    camg[me] = camt[pl.ds(pl.multiple_of(me * part, 16), part), :]
+    if not fused:
+        for i in range(1, n):
+            peer = lax.rem(me + i, n)
+            start = pl.multiple_of(peer * part, 16)
+            copy = remote(camt.at[pl.ds(start, part)], camg.at[me], cs.at[i], cr.at[i], mf, peer)
+            copy.start()
+            columns.append(copy)
+        camg[me] = camt[pl.ds(pl.multiple_of(me * part, 16), part), :]
 
     loads[2].wait()
     depth = refs * unit
@@ -198,66 +208,103 @@
     ).astype(F32).astype(BF16)
     for copy in returns:
         copy.wait_recv()
-    gall[me] = dot(home, back[...].reshape(slot_rows, head)).astype(BF16)
-
+    row_grads = dot(home, back[...].reshape(slot_rows, head)).astype(BF16)
+    pending = forward + returns
     nz = n // 2
     z = me // 2
     core = lax.rem(me, 2)
     twin = z * 2 + (1 - core)
-    gathers = [None]
-    for i in range(1, nz):
-        peer = lax.rem(z + i, nz) * 2 + core
-        copy = remote(gall.at[me], gall.at[me], gs_sem.at[i], gr_sem.at[i], mf, peer)
-        copy.start()
-        gathers.append(copy)
-    passed = [remote(gall.at[me], gall.at[me], ps.at[0], pr.at[0], mf, twin)]
-    passed[0].start()
-    for copy in columns:
-        copy.wait_recv()
-    acc[...] = dot(camg[me], gall[me])
-    for i in range(1, nz):
-        source = lax.rem(z + nz - i, nz) * 2 + core
-        gathers[i].wait_recv()
-        copy = remote(gall.at[source], gall.at[source], ps.at[i], pr.at[i], mf, twin)
-        copy.start()
-        passed.append(copy)
-        acc[...] += dot(camg[source], gall[source])
-    for i in range(nz):
-        source = lax.rem(z + nz - i, nz) * 2 + (1 - core)
-        passed[i].wait_recv()
-        acc[...] += dot(camg[source], gall[source])
-
-    pending = forward + columns + returns + gathers[1:] + passed
     if fused:
         quarter = part // nf
-        rsend[...] = acc[...].astype(BF16)
-        sums = []
-        for i in range(1, nf):
-            peer = lax.rem(mf + i, nf)
-            start = pl.multiple_of(peer * quarter, 16)
-            copy = remote(
-                rsend.at[pl.ds(start, quarter)], rrecv.at[i], xs.at[i], xr.at[i], peer, me
-            )
+        order = [lax.rem(z + i, nz) for i in range(1, nz)] + [z]
+
+        def term(zz, c):
+            start = pl.multiple_of((zz * 2 + c) * part, 16)
+            return dot(camt[pl.ds(start, part), :], row_grads)
+
+        swaps = []
+        for i, zz in enumerate(order):
+            give[i] = term(zz, 1 - core).astype(BF16)
+            copy = remote(give.at[i], got.at[i], es.at[i], er.at[i], mf, twin)
             copy.start()
-            sums.append(copy)
-        total = acc[pl.ds(pl.multiple_of(mf * quarter, 16), quarter), :]
-        for i in range(1, nf):
-            sums[i - 1].wait_recv()
-            total = total + rrecv[i].astype(F32)
+            swaps.append(copy)
+        for i, zz in enumerate(order):
+            keep[i] = term(zz, core)
+        scatters = []
+        for i in range(nz):
+            swaps[i].wait_recv()
+            pair = keep[i] + got[i].astype(F32)
+            keep[i] = pair
+            fsend[i] = pair.astype(BF16)
+            for j in range(1, nf):
+                peer = lax.rem(mf + j, nf)
+                start = pl.multiple_of(peer * quarter, 16)
+                copy = remote(
+                    fsend.at[i, pl.ds(start, quarter)],
+                    frecv.at[i, j],
+                    xs.at[i, j],
+                    xr.at[i, j],
+                    peer,
+                    me,
+                )
+                copy.start()
+                scatters.append(copy)
+        climbs = []
+        mine = pl.ds(pl.multiple_of(mf * quarter, 16), quarter)
+        for i, zz in enumerate(order):
+            total = keep[i, mine, :]
+            for j in range(1, nf):
+                scatters[i * (nf - 1) + j - 1].wait_recv()
+                total = total + frecv[i, j].astype(F32)
+            if i < nz - 1:
+                zsend[i] = total.astype(BF16)
+                copy = remote(
+                    zsend.at[i], zrecv.at[i], zs.at[i], zr.at[i], mf, zz * 2 + core
+                )
+                copy.start()
+                climbs.append(copy)
+        for i, copy in enumerate(climbs):
+            copy.wait_recv()
+            total = total + zrecv[i].astype(F32)
         fgat[mf] = total.astype(BF16)
         spreads = []
-        for i in range(1, nf):
-            peer = lax.rem(mf + i, nf)
-            copy = remote(fgat.at[mf], fgat.at[mf], ys.at[i], yr.at[i], peer, me)
+        for j in range(1, nf):
+            peer = lax.rem(mf + j, nf)
+            copy = remote(fgat.at[mf], fgat.at[mf], ys.at[j], yr.at[j], peer, me)
             copy.start()
             spreads.append(copy)
         for copy in spreads:
             copy.wait_recv()
         for f in range(nf):
-            gh[f * quarter : (f + 1) * quarter, :] = fgat[f].astype(F32)
-        pending = pending + sums + spreads
+            gh[f * quarter : (f + 1) * quarter, :] = fgat[f]
+        pending += swaps + scatters + climbs + spreads
     else:
+        gall[me] = row_grads
+        gathers = [None]
+        for i in range(1, nz):
+            peer = lax.rem(z + i, nz) * 2 + core
+            copy = remote(gall.at[me], gall.at[me], gs_sem.at[i], gr_sem.at[i], mf, peer)
+            copy.start()
+            gathers.append(copy)
+        passed = [remote(gall.at[me], gall.at[me], ps.at[0], pr.at[0], mf, twin)]
+        passed[0].start()
+        for copy in columns:
+            copy.wait_recv()
+        acc[...] = dot(camg[me], gall[me])
+        for i in range(1, nz):
+            source = lax.rem(z + nz - i, nz) * 2 + core
+            gathers[i].wait_recv()
+            copy = remote(gall.at[source], gall.at[source], ps.at[i], pr.at[i], mf, twin)
+            copy.start()
+            passed.append(copy)
+            acc[...] += dot(camg[source], gall[source])
+        for i in range(nz):
+            source = lax.rem(z + nz - i, nz) * 2 + (1 - core)
+            passed[i].wait_recv()
+            acc[...] += dot(camg[source], gall[source])
+
         gh[...] = acc[...]
+        pending += columns + gathers[1:] + passed
     for copy in pending:
         copy.wait_send()
     for store in stores:
@@ -278,15 +325,20 @@
     part = width // n
     fused = part % (nf * 16) == 0
     quarter = part // nf if fused else 16
+    nz = n // 2 if fused else 1
+
+    def tall(size):
+        return 1 if fused else size
+
     sizes = (n, nf, units, unit, blocks, refs, lbr, fused)
-    any_space = pl.BlockSpec(memory_space=pl.ANY)
+    any_space = pl.BlockSpec(memory_space=pltpu.HBM)
     smem = pl.BlockSpec(memory_space=pltpu.SMEM)
     dma = pltpu.SemaphoreType.DMA
     grad_student, grad_head = pl.pallas_call(
         functools.partial(kernel_body, sizes),
         out_shape=(
             jax.ShapeDtypeStruct((tokens, head), BF16),
-            jax.ShapeDtypeStruct((part, head), F32),
+            jax.ShapeDtypeStruct((part, head), BF16 if fused else F32),
         ),
         in_specs=[smem, smem, any_space, any_space, any_space, any_space],
         out_specs=(any_space, pl.BlockSpec(memory_space=pltpu.VMEM)),
@@ -298,17 +350,22 @@
             pltpu.VMEM((n, CAP * unit, head), BF16),
             pltpu.VMEM((n, CAP * unit, head), BF16),
             pltpu.VMEM((width, rows), BF16),
-            pltpu.VMEM((n, part, rows), BF16),
+            pltpu.VMEM((tall(n), part, rows), BF16),
             pltpu.VMEM((slot_rows, tokens), BF16),
             pltpu.VMEM((tokens, slot_rows), BF16),
             pltpu.VMEM((tokens, head), BF16),
             pltpu.VMEM((tokens, head), BF16),
             pltpu.VMEM((n, CAP * unit, head), BF16),
             pltpu.VMEM((n, CAP * unit, head), BF16),
-            pltpu.VMEM((n, rows, head), BF16),
+            pltpu.VMEM((tall(n), rows, head), BF16),
             pltpu.VMEM((part, head), F32),
-            pltpu.VMEM((part, head), BF16),
-            pltpu.VMEM((nf, quarter, head), BF16),
+            pltpu.VMEM((nz, part, head), BF16),
+            pltpu.VMEM((nz, part, head), BF16),
+            pltpu.VMEM((nz, part, head), F32),
+            pltpu.VMEM((nz, part, head), BF16),
+            pltpu.VMEM((nz, nf, quarter, head), BF16),
+            pltpu.VMEM((nz, quarter, head), BF16),
+            pltpu.VMEM((nz, quarter, head), BF16),
             pltpu.VMEM((nf, quarter, head), BF16),
             dma((4,)),
             dma((blocks,)),
@@ -322,13 +379,17 @@
             dma((n,)),
             dma((n,)),
             dma((n,)),
-            dma((nf,)),
-            dma((nf,)),
+            dma((nz,)),
+            dma((nz,)),
+            dma((nz, nf)),
+            dma((nz, nf)),
+            dma((nz,)),
+            dma((nz,)),
             dma((nf,)),
             dma((nf,)),
         ],
         compiler_params=pltpu.CompilerParams(
-            collective_id=0, has_side_effects=True, vmem_limit_bytes=48 * 1024 * 1024
+            collective_id=0, has_side_effects=True, vmem_limit_bytes=60 * 1024 * 1024
         ),
     )(
         owners,
@@ -338,7 +399,9 @@
         student,
         head_weight,
     )
-    if not fused:
+    if fused:
+        grad_head = grad_head.astype(F32)
+    else:
         grad_head = lax.psum(grad_head, "frame")
     return (grad_student, grad_head)
 

time: 57.7 us -> 45.4 us (0.79)
  Pallas kernels: 49.2 us -> 40.5 us
  local copies, waits for them, and re-layouts: 7.63 us -> 2.26 us
  other arithmetic: 0 us -> 1.72 us
    pallas_call x1, Pallas kernels: 49.2 us -> 40.5 us  [on_device(): pl.pallas_call(functools.partial(kernel_body, sizes), out_shape=(jax.Shap...]
    unnamed x14 -> x1, local copies, waits for them, and re-layouts: 7.63 us -> 2.26 us
    convert_element_type x0 -> x1, other arithmetic: none -> 1.72 us  [on_device(): grad_head = grad_head.astype(F32)]
where the time goes in v2:
time: 45.4 us; the launch traced here: 45.2 us
  Pallas kernels  40.5 us (89%)
  local copies, waits for them, and re-layouts  2.26 us (5%)
  other arithmetic  1.72 us (4%)
  between operations  0.64 us (1%)
    pallas_call x1, Pallas kernels, on_device(): pl.pallas_call(functools.partial(kernel_body, sizes), out_shape=(jax.Shap...  40.5 us
    unnamed x1, local copies, waits for them, and re-layouts  2.26 us
    convert_element_type x1, other arithmetic, on_device(): grad_head = grad_head.astype(F32)  1.72 us

profile of v2, /device:TPU:0, one launch (start us, length us, event | category | flops | bytes accessed | tf_op | source)
XLA Modules:
  0.0 45.2 jit_solution(3347599906380376685)
XLA Ops:
  0.6 40.5 %shard_map.77 = (bf16[1024,512]{1,0:T(8,128)(2,1)}, bf16[192,512]{1,0:T(8,128)(2,1)}) custom-call(s32[8]{0:T(128)} %owners.1, s32[8,8]{1,0:T(8,128)} %slots.1, bf16[128,1536]{1,0:T(8,128)(2,1)} %cam_h.1, bf16[1024,128]{1,0:T(8,128)(2,1)} %bitcast.1, bf16[1024,512]{1,0:T(8,128)(2,1)} %stu_h.1, bf16[1536,512]{1,0:T(8,128)(2,1)} %w_h.1), custom_call_target="tpu_custom_call" | custom-call | tf_op jit(solution)/shard_map/pallas_call | solution.py:337
  41.2 1.7 %convert_element_type.3 = f32[192,512]{1,0:T(8,128)} convert(bf16[192,512]{1,0:T(8,128)(2,1)} %get-tuple-element.5) | non-fusion elementwise | flops 98304 | bytes 589824 | tf_op jit(solution)/shard_map/convert_element_type | solution.py:403
  42.9 2.3 %copy.9 = bf16[1024,512]{1,0:T(8,128)(2,1)} copy(bf16[1024,512]{1,0:T(8,128)(2,1)} %get-tuple-element.8) | data formatting | bytes 2097152

commit v3 on v2

--- a/solution.py
+++ b/solution.py
@@ -26,7 +26,7 @@
     pool_h,
     stu_h,
     w_h,
-    gs_h,
+    gs,
     gh,
     cam,
     pool,
@@ -39,7 +39,6 @@
     bmat,
     bt,
     gt,
-    gsv,
     sg,
     back,
     gall,
@@ -53,7 +52,6 @@
     zrecv,
     fgat,
     load_sem,
-    store_sem,
     fs,
     fr,
     cs,
@@ -172,7 +170,6 @@
     for copy in forward:
         copy.wait_recv()
     arrived = recv[...].reshape(slot_rows, head)
-    stores = []
     for b in range(blocks):
         span = slice(b * lbr, (b + 1) * lbr)
         target = dot(bt[span, :], arrived)
@@ -184,11 +181,8 @@
         scale = -LOSS_WEIGHT * both
         back_l = LOSS_WEIGHT * cosine * (inv_l * inv_l)
         back_t = LOSS_WEIGHT * cosine * (inv_t * inv_t)
-        gsv[span, :] = (target * scale + learner * back_l).astype(BF16)
+        gs[span, :] = (target * scale + learner * back_l).astype(BF16)
         gt[span, :] = (learner * scale + target * back_t).astype(BF16)
-        store = pltpu.make_async_copy(gsv.at[span], gs_h.at[span], store_sem.at[b])
-        store.start()
-        stores.append(store)
 
     sg[...] = dot(bmat[...], gt[...]).astype(BF16).reshape(n, CAP * unit, head)
     returns = []
@@ -307,8 +301,6 @@
         pending += columns + gathers[1:] + passed
     for copy in pending:
         copy.wait_send()
-    for store in stores:
-        store.wait()
 
 
 def on_device(camera, owners, unit_slots, pool_weights, student, head_weight):
@@ -341,7 +333,7 @@
             jax.ShapeDtypeStruct((part, head), BF16 if fused else F32),
         ),
         in_specs=[smem, smem, any_space, any_space, any_space, any_space],
-        out_specs=(any_space, pl.BlockSpec(memory_space=pltpu.VMEM)),
+        out_specs=(pl.BlockSpec(memory_space=pltpu.VMEM), pl.BlockSpec(memory_space=pltpu.VMEM)),
         scratch_shapes=[
             pltpu.VMEM((rows, width), BF16),
             pltpu.VMEM((blocks * refs * unit, lbr), BF16),
@@ -353,7 +345,6 @@
             pltpu.VMEM((tall(n), part, rows), BF16),
             pltpu.VMEM((slot_rows, tokens), BF16),
             pltpu.VMEM((tokens, slot_rows), BF16),
-            pltpu.VMEM((tokens, head), BF16),
             pltpu.VMEM((tokens, head), BF16),
             pltpu.VMEM((n, CAP * unit, head), BF16),
             pltpu.VMEM((n, CAP * unit, head), BF16),
@@ -368,7 +359,6 @@
             pltpu.VMEM((nz, quarter, head), BF16),
             pltpu.VMEM((nf, quarter, head), BF16),
             dma((4,)),
-            dma((blocks,)),
             dma((n,)),
             dma((n,)),
             dma((n,)),
@@ -389,15 +379,20 @@
             dma((nf,)),
         ],
         compiler_params=pltpu.CompilerParams(
-            collective_id=0, has_side_effects=True, vmem_limit_bytes=60 * 1024 * 1024
+            collective_id=0, has_side_effects=True, vmem_limit_bytes=40 * 1024 * 1024
         ),
     )(
-        owners,
-        unit_slots,
-        camera,
-        pool_weights.reshape(blocks * refs * unit, lbr),
-        student,
-        head_weight,
+        *(
+            pltpu.with_memory_space_constraint(x, pltpu.HBM)
+            for x in (
+                owners,
+                unit_slots,
+                camera,
+                pool_weights.reshape(blocks * refs * unit, lbr),
+                student,
+                head_weight,
+            )
+        ),
     )
     if fused:
         grad_head = grad_head.astype(F32)

time: 45.4 us -> 42.4 us (0.934)
  local copies, waits for them, and re-layouts: 2.26 us -> 0.97 us
  other arithmetic: 1.72 us -> 0.79 us
  Pallas kernels: 40.5 us -> 39.8 us
    unnamed x1, local copies, waits for them, and re-layouts: 2.26 us -> 0.97 us
    convert_element_type x1, other arithmetic: 1.72 us -> 0.79 us  [on_device(): grad_head = grad_head.astype(F32)]
    pallas_call x1, Pallas kernels: 40.5 us -> 39.8 us  [on_device(): pl.pallas_call(functools.partial(kernel_body, sizes), out_shape=(jax.Shap...]
where the time goes in v3:
time: 42.4 us; the launch traced here: 42.2 us
  Pallas kernels  39.8 us (94%)
  local copies, waits for them, and re-layouts  0.97 us (2%)
  other arithmetic  0.79 us (2%)
  between operations  0.64 us (2%)
    pallas_call x1, Pallas kernels, on_device(): pl.pallas_call(functools.partial(kernel_body, sizes), out_shape=(jax.Shap...  39.8 us
    unnamed x1, local copies, waits for them, and re-layouts  0.97 us

profile of v3, /device:TPU:0, one launch (start us, length us, event | category | flops | bytes accessed | tf_op | source)
XLA Modules:
  0.0 42.2 jit_solution(2608541884823317543)
XLA Ops:
  0.6 39.8 %shard_map.77 = (bf16[1024,512]{1,0:T(8,128)(2,1)S(1)}, bf16[192,512]{1,0:T(8,128)(2,1)S(1)}) custom-call(s32[8]{0:T(128)} %owners.1, s32[8,8]{1,0:T(8,128)} %slots.1, bf16[128,1536]{1,0:T(8,128)(2,1)} %cam_h.1, bf16[1024,128]{1,0:T(8,128)(2,1)} %bitcast.1, bf16[1024,512]{1,0:T(8,128)(2,1)} %stu_h.1, bf16[1536,512]{1,0:T(8,128)(2,1)} %w_h.1), custom_call_target="tpu_custom_call" | custom-call | tf_op jit(solution)/shard_map/pallas_call | solution.py:329
  40.4 0.8 %convert_element_type.3 = f32[192,512]{1,0:T(8,128)} convert(bf16[192,512]{1,0:T(8,128)(2,1)S(1)} %get-tuple-element.5) | non-fusion elementwise | flops 98304 | bytes 589824 | tf_op jit(solution)/shard_map/convert_element_type | solution.py:398
  41.2 1.0 %copy.9 = bf16[1024,512]{1,0:T(8,128)(2,1)} copy(bf16[1024,512]{1,0:T(8,128)(2,1)S(1)} %get-tuple-element.8) | data formatting | bytes 2097152

commit v4 on v3

--- a/solution.py
+++ b/solution.py
@@ -20,14 +20,16 @@
 
 def kernel_body(
     sizes,
-    owners,
-    slots,
+    owners_h,
+    slots_h,
     cam_h,
     pool_h,
     stu_h,
     w_h,
     gs,
     gh,
+    owners,
+    slots,
     cam,
     pool,
     stu,
@@ -79,13 +81,6 @@
     me = lax.axis_index("sector")
     mf = lax.axis_index("frame")
 
-    loads = [
-        pltpu.make_async_copy(src, dst, load_sem.at[i])
-        for i, (src, dst) in enumerate(((cam_h, cam), (w_h, w), (pool_h, pool), (stu_h, stu)))
-    ]
-    for copy in loads:
-        copy.start()
-
     def remote(src, dst, ssem, rsem, frame, sector):
         return pltpu.make_async_remote_copy(
             src_ref=src,
@@ -112,6 +107,24 @@
             )
         greeted += nf - 1
 
+    loads = [
+        pltpu.make_async_copy(src, dst, load_sem.at[i])
+        for i, (src, dst) in enumerate(
+            (
+                (cam_h, cam),
+                (w_h, w),
+                (pool_h, pool),
+                (stu_h, stu),
+                (owners_h, owners),
+                (slots_h, slots),
+            )
+        )
+    ]
+    for copy in loads[4:] + loads[:4]:
+        copy.start()
+
+    loads[4].wait()
+    loads[5].wait()
     dest = []
     for u in range(units):
         rank = jnp.int32(0)
@@ -217,32 +230,34 @@
             return dot(camt[pl.ds(start, part), :], row_grads)
 
         swaps = []
-        for i, zz in enumerate(order):
-            give[i] = term(zz, 1 - core).astype(BF16)
-            copy = remote(give.at[i], got.at[i], es.at[i], er.at[i], mf, twin)
-            copy.start()
-            swaps.append(copy)
-        for i, zz in enumerate(order):
-            keep[i] = term(zz, core)
         scatters = []
-        for i in range(nz):
-            swaps[i].wait_recv()
-            pair = keep[i] + got[i].astype(F32)
-            keep[i] = pair
-            fsend[i] = pair.astype(BF16)
+        for i in range(nz + 1):
+            if i < nz:
+                give[i] = term(order[i], 1 - core).astype(BF16)
+                copy = remote(give.at[i], got.at[i], es.at[i], er.at[i], mf, twin)
+                copy.start()
+                swaps.append(copy)
+            if i == 0:
+                continue
+            k = i - 1
+            kept = term(order[k], core)
+            swaps[k].wait_recv()
+            pair = kept + got[k].astype(F32)
+            fsend[k] = pair.astype(BF16)
             for j in range(1, nf):
                 peer = lax.rem(mf + j, nf)
                 start = pl.multiple_of(peer * quarter, 16)
                 copy = remote(
-                    fsend.at[i, pl.ds(start, quarter)],
-                    frecv.at[i, j],
-                    xs.at[i, j],
-                    xr.at[i, j],
+                    fsend.at[k, pl.ds(start, quarter)],
+                    frecv.at[k, j],
+                    xs.at[k, j],
+                    xr.at[k, j],
                     peer,
                     me,
                 )
                 copy.start()
                 scatters.append(copy)
+            keep[k] = pair
         climbs = []
         mine = pl.ds(pl.multiple_of(mf * quarter, 16), quarter)
         for i, zz in enumerate(order):
@@ -324,7 +339,6 @@
 
     sizes = (n, nf, units, unit, blocks, refs, lbr, fused)
     any_space = pl.BlockSpec(memory_space=pltpu.HBM)
-    smem = pl.BlockSpec(memory_space=pltpu.SMEM)
     dma = pltpu.SemaphoreType.DMA
     grad_student, grad_head = pl.pallas_call(
         functools.partial(kernel_body, sizes),
@@ -332,9 +346,11 @@
             jax.ShapeDtypeStruct((tokens, head), BF16),
             jax.ShapeDtypeStruct((part, head), BF16 if fused else F32),
         ),
-        in_specs=[smem, smem, any_space, any_space, any_space, any_space],
+        in_specs=[any_space, any_space, any_space, any_space, any_space, any_space],
         out_specs=(pl.BlockSpec(memory_space=pltpu.VMEM), pl.BlockSpec(memory_space=pltpu.VMEM)),
         scratch_shapes=[
+            pltpu.SMEM(owners.shape, jnp.int32),
+            pltpu.SMEM(unit_slots.shape, jnp.int32),
             pltpu.VMEM((rows, width), BF16),
             pltpu.VMEM((blocks * refs * unit, lbr), BF16),
             pltpu.VMEM((tokens, head), BF16),
@@ -358,7 +374,7 @@
             pltpu.VMEM((nz, quarter, head), BF16),
             pltpu.VMEM((nz, quarter, head), BF16),
             pltpu.VMEM((nf, quarter, head), BF16),
-            dma((4,)),
+            dma((6,)),
             dma((n,)),
             dma((n,)),
             dma((n,)),

time: 42.4 us -> 41.9 us (0.988)
  Pallas kernels: 39.8 us -> 39.3 us
    pallas_call x1, Pallas kernels: 39.8 us -> 39.3 us  [on_device(): pl.pallas_call(functools.partial(kernel_body, sizes), out_shape=(jax.Shap...]
where the time goes in v4:
time: 41.9 us; the launch traced here: 41.7 us
  Pallas kernels  39.3 us (94%)
  local copies, waits for them, and re-layouts  0.97 us (2%)
  other arithmetic  0.79 us (2%)
  between operations  0.64 us (2%)
    pallas_call x1, Pallas kernels, on_device(): pl.pallas_call(functools.partial(kernel_body, sizes), out_shape=(jax.Shap...  39.3 us
    unnamed x1, local copies, waits for them, and re-layouts  0.97 us

profile of v4, /device:TPU:0, one launch (start us, length us, event | category | flops | bytes accessed | tf_op | source)
XLA Modules:
  0.0 41.7 jit_solution(11750906203970238605)
XLA Ops:
  0.6 39.3 %shard_map.77 = (bf16[1024,512]{1,0:T(8,128)(2,1)S(1)}, bf16[192,512]{1,0:T(8,128)(2,1)S(1)}) custom-call(s32[8]{0:T(128)} %owners_h.1, s32[8,8]{1,0:T(8,128)} %slots_h.1, bf16[128,1536]{1,0:T(8,128)(2,1)} %cam_h.1, bf16[1024,128]{1,0:T(8,128)(2,1)} %bitcast.1, bf16[1024,512]{1,0:T(8,128)(2,1)} %stu_h.1, bf16[1536,512]{1,0:T(8,128)(2,1)} %w_h.1), custom_call_target="tpu_custom_call" | custom-call | tf_op jit(solution)/shard_map/pallas_call | solution.py:343
  40.0 0.8 %convert_element_type.3 = f32[192,512]{1,0:T(8,128)} convert(bf16[192,512]{1,0:T(8,128)(2,1)S(1)} %get-tuple-element.5) | non-fusion elementwise | flops 98304 | bytes 589824 | tf_op jit(solution)/shard_map/convert_element_type | solution.py:414
  40.8 1.0 %copy.9 = bf16[1024,512]{1,0:T(8,128)(2,1)} copy(bf16[1024,512]{1,0:T(8,128)(2,1)S(1)} %get-tuple-element.8) | data formatting | bytes 2097152

commit v5 on v4

--- a/solution.py
+++ b/solution.py
@@ -183,6 +183,7 @@
     for copy in forward:
         copy.wait_recv()
     arrived = recv[...].reshape(slot_rows, head)
+    scales = []
     for b in range(blocks):
         span = slice(b * lbr, (b + 1) * lbr)
         target = dot(bt[span, :], arrived)
@@ -194,7 +195,7 @@
         scale = -LOSS_WEIGHT * both
         back_l = LOSS_WEIGHT * cosine * (inv_l * inv_l)
         back_t = LOSS_WEIGHT * cosine * (inv_t * inv_t)
-        gs[span, :] = (target * scale + learner * back_l).astype(BF16)
+        scales.append((scale, back_l))
         gt[span, :] = (learner * scale + target * back_t).astype(BF16)
 
     sg[...] = dot(bmat[...], gt[...]).astype(BF16).reshape(n, CAP * unit, head)
@@ -205,6 +206,11 @@
         copy.start()
         returns.append(copy)
     back[me] = sg[me]
+    for b in range(blocks):
+        span = slice(b * lbr, (b + 1) * lbr)
+        scale, back_l = scales[b]
+        target = dot(bt[span, :], recv[...].reshape(slot_rows, head))
+        gs[span, :] = (target * scale + stu[span, :].astype(F32) * back_l).astype(BF16)
 
     place_column = lax.broadcasted_iota(jnp.int32, (rows, 1), 0)
     home_row = lax.rem(place_column, unit)

time: 41.9 us -> 41.6 us (level)
  no operation moved by 1% of the time
where the time goes in v5:
time: 41.6 us; the launch traced here: 41.4 us
  Pallas kernels  39 us (94%)
  local copies, waits for them, and re-layouts  0.97 us (2%)
  other arithmetic  0.79 us (2%)
  between operations  0.64 us (2%)
    pallas_call x1, Pallas kernels, on_device(): pl.pallas_call(functools.partial(kernel_body, sizes), out_shape=(jax.Shap...  39 us
    unnamed x1, local copies, waits for them, and re-layouts  0.97 us

profile of v5, /device:TPU:0, one launch (start us, length us, event | category | flops | bytes accessed | tf_op | source)
XLA Modules:
  0.0 41.4 jit_solution(12539327131832954659)
XLA Ops:
  0.6 39.0 %shard_map.77 = (bf16[1024,512]{1,0:T(8,128)(2,1)S(1)}, bf16[192,512]{1,0:T(8,128)(2,1)S(1)}) custom-call(s32[8]{0:T(128)} %owners_h.1, s32[8,8]{1,0:T(8,128)} %slots_h.1, bf16[128,1536]{1,0:T(8,128)(2,1)} %cam_h.1, bf16[1024,128]{1,0:T(8,128)(2,1)} %bitcast.1, bf16[1024,512]{1,0:T(8,128)(2,1)} %stu_h.1, bf16[1536,512]{1,0:T(8,128)(2,1)} %w_h.1), custom_call_target="tpu_custom_call" | custom-call | tf_op jit(solution)/shard_map/pallas_call | solution.py:349
  39.7 0.8 %convert_element_type.3 = f32[192,512]{1,0:T(8,128)} convert(bf16[192,512]{1,0:T(8,128)(2,1)S(1)} %get-tuple-element.5) | non-fusion elementwise | flops 98304 | bytes 589824 | tf_op jit(solution)/shard_map/convert_element_type | solution.py:420
  40.4 1.0 %copy.9 = bf16[1024,512]{1,0:T(8,128)(2,1)} copy(bf16[1024,512]{1,0:T(8,128)(2,1)S(1)} %get-tuple-element.8) | data formatting | bytes 2097152
